TPU v7x, 32 devices: a whole 2x2x4 slice. The times are simulated.
32 devices in a mesh: subj: 2 (over x), row: 8 (over z, y), col: 2 (over core).
Axes of the slice: x: 2, y: 2, z: 4, core: 2. Of those that a mesh axis runs over, the one named last changes fastest.
Arguments:
- series: float32 [256, 11392], P(('subj', 'row', 'col')), parts along dimension 0, may hold values from -30 to 30
- tap_values: float32 [17], replicated, may hold values from -4 to 4
- tap_count: int32 [1], replicated, may hold values from 4 to 8
- kept_frames: int32 [32], P('subj'), parts along dimension 0, may hold values from 1 to 8, 96 in all
- band_start: int32 [2], P('subj'), parts along dimension 0, may hold values from 0 to 7296
Outputs:
- fisher_band: bfloat16 [8192, 11392], P('subj', ('row', 'col')), parts along dimension 0
There are 2 independent parts, one for each index of `subj`. A program takes and returns all parts, laid end to end along the dimension named above; an argument that names none is the same for every part. Nothing has to cross between parts.
Inputs may be any that keep to these rules, and one draw needn't show every extreme that they name: `tap_count`: frames farther than this from the centre get no weight. Time block d holds frames d * 8 to (d + 1) * 8 - 1; only its first kept_frames[d] frames are kept. `band_start`: the 4096 band grayordinates lie inside the grid.
All inputs are finite; a program needn't handle non-finite values.
Results may differ from a plain program's by a relative error of at most 0.0031.
The roundings to bfloat16 on the way count: a program that leaves them out, or rounds other values in their place, can miss the bound.
Values may be sent and summed in bfloat16 or wider, within the bound.
No kernel may reach another device: no remote copies, remote signals or barrier semaphores. Data moves between devices by JAX's collectives and lax.ppermute only.
A program may use at most 128 MiB of HBM per device.

v0:
```python
import jax
import jax.numpy as jnp
from jax import lax
from jax.sharding import PartitionSpec as P

B = 4096
EPSILON = 1e-06
CLIP_LIMIT = 0.999


def with_halo(cells, sides, width):
    for axis, dim in sides:
        count = lax.axis_size(axis)
        ends = count - 1
        head = lax.slice_in_dim(cells, 0, width, axis=dim)
        tail = lax.slice_in_dim(cells, cells.shape[dim] - width, cells.shape[dim], axis=dim)
        cells = jnp.concatenate(
            [
                lax.ppermute(tail, axis, [(i, (i + 1) % count) for i in range(ends)]),
                cells,
                lax.ppermute(head, axis, [((i + 1) % count, i) for i in range(ends)]),
            ],
            axis=dim,
        )
    return cells


def tap_table(tap_values, tap_count):
    tap_reach = tap_values.shape[0] // 2
    offsets = jnp.arange(tap_values.shape[0], dtype=jnp.int32) - tap_reach
    active = (jnp.abs(offsets) <= tap_count[0]).astype(jnp.float32)
    centre = jnp.sum(active * tap_values) / jnp.sum(active)
    return active * (tap_values - centre)


def band_filter(padded, tap_weights, length):
    filtered = tap_weights[0] * padded[0:length]
    for tap_index in range(1, tap_weights.shape[0]):
        filtered = filtered + tap_weights[tap_index] * padded[tap_index : tap_index + length]
    return filtered


def fisher_z(correlation):
    clipped = jnp.clip(correlation, -CLIP_LIMIT, CLIP_LIMIT)
    return 0.5 * (jnp.log1p(clipped) - jnp.log1p(-clipped))


def body(series, tap_values, tap_count, kept_frames, band_start):
    tap_reach = tap_values.shape[0] // 2
    tap_weights = tap_table(tap_values, tap_count)
    block_len = series.shape[0]
    padded = with_halo(series, ((("row", "col"), 0),), tap_reach)
    filtered = band_filter(padded, tap_weights, block_len)
    own_kept = kept_frames[lax.axis_index(("row", "col"))]
    keep_mask = (jnp.arange(block_len, dtype=jnp.int32) < own_kept).astype(jnp.float32)[:, None]
    centered = keep_mask * filtered
    spread = lax.psum(jnp.sum(centered * centered, axis=0), ("row", "col"))
    scaled = (centered * lax.rsqrt(spread + EPSILON)).astype(jnp.bfloat16)
    columns = lax.all_to_all(scaled, ("row", "col"), split_axis=1, concat_axis=0, tiled=True)
    band_slice = lax.dynamic_slice_in_dim(scaled, band_start[0], B, 1)
    band_cols = lax.all_gather(band_slice, ("row", "col"), axis=0, tiled=True)
    correlation = lax.dot_general(
        band_cols, columns, (((0,), (0,)), ((), ())), preferred_element_type=jnp.float32
    )
    return fisher_z(correlation).astype(jnp.bfloat16)


def solution(mesh):
    placed = (P(("subj", "row", "col"), None), P(), P(), P("subj"), P("subj"))
    return jax.shard_map(
        body, mesh=mesh, in_specs=placed, out_specs=P("subj", ("row", "col")), check_vma=False
    )
```

profile of v0, /device:TPU:0, one launch (start us, length us, event | category | flops | bytes accessed | tf_op | source)
XLA Modules:
  0.0 151.6 jit_solution(5790544908060387476)
XLA Ops:
  6.5 0.0 all-gather.2.cloned.1.call-start
  6.5 2.4 %collective-permute-start = (f32[8,11392]{1,0:T(8,128)}, f32[8,11392]{1,0:T(8,128)S(1)}, u32[]{:S(2)}, u32[]{:S(2)}) collective-permute-start(f32[8,11392]{1,0:T(8,128)} %param.5), channel_id=1, source_target_pairs={{0,1},{1,2},{2,3},{3,4},{4,5},{5,6},{6,7},{7,8},{8,9},{9,10},{10,1... | collective-permute-start | bytes 1093640 | tf_op jit(solution)/shard_map/ppermute | solution.py:19
  8.9 1.3 collective-permute-start.1
  10.9 1.3 dynamic_slice.6
  12.1 1.3 convert_reduce_fusion
  13.5 0.6 compare_convert_fusion
  16.1 0.7 subtract_select_fusion
  16.7 0.7 fusion.19
  17.4 0.0 collective-permute-done
  17.5 1.0 constant_dynamic-update-slice_fusion
  18.5 0.0 collective-permute-done.1
  18.6 12.4 %multiply_reduce_fusion = (f32[11392]{0:T(1024)S(1)}, f32[8,11392]{1,0:T(8,128)S(1)}) fusion(f32[8,11392]{1,0:T(8,128)S(1)} %collective-permute-done.1, f32[]{:T(128)} %bitcast.18, f32[16,11392]{1,0:T(8,128)S(1)} %constant_dynamic-update-slice_fusion.2, f32[]{:T(128)} %bitcast.17, f32[]{:T(128)} %bitcast.16, f32[]{:T(128)} %bitcast.15, f32[]{:T(128)} %bitcast.14, ...), kind=kLoop, calls=%fused_computation.33 | loop fusion | flops 3269504 | bytes 6607460 | tf_op jit(solution)/shard_map/reduce_sum | solution.py:57
  31.0 63.9 %psum.7 = f32[11392]{0:T(1024)S(1)} all-reduce(f32[11392]{0:T(1024)S(1)} %get-tuple-element.5), channel_id=1, replica_groups=mesh['subj'=2,'row'=8,'col'=2] {'row','col'}, use_global_device_ids=true, to_apply=%region_3.0 | all-reduce | flops 11392 | bytes 91136 | tf_op jit(solution)/shard_map/psum | solution.py:57
  94.9 0.7 constant_dynamic-slice_fusion
  95.7 0.0 all-gather.2.cloned.1.call-update
  95.7 0.4 all_to_all.14
  96.1 0.1 copy.6
  96.2 12.3 %all_to_all.19 = bf16[8,16,712]{2,0,1:T(8,128)(2,1)S(1)} all-to-all(bf16[8,16,712]{2,0,1:T(8,128)(2,1)S(1)} %copy.6), channel_id=1, replica_groups=mesh['subj'=2,'row'=8,'col'=2] {'row','col'}, dimensions={1} | all-to-all | bytes 364544 | tf_op jit(solution)/shard_map/all_to_all | solution.py:59
  108.5 23.6 %all-gather.2.cloned.1.call-done = bf16[128,4096]{1,0:T(8,128)(2,1)} async-done(((bf16[8,4096]{1,0:T(8,128)(2,1)}), bf16[128,4096]{1,0:T(8,128)(2,1)}) %all-gather.2.cloned.1.call-update) | async-done | bytes 1048592 | tf_op jit(solution)/shard_map/all_gather | solution.py:61
  132.1 12.7 %multiply_convert_fusion = bf16[4096,712]{0,1:T(8,128)(2,1)} fusion(bf16[128,4096]{1,0:T(8,128)(2,1)} %all-gather.2.cloned.1.call-done, bf16[8,16,712]{2,0,1:T(8,128)(2,1)S(1)} %all_to_all.19), kind=kOutput, calls=%fused_computation | convolution fusion | flops 761167872 | bytes 7063552 | tf_op jit(solution)/shard_map/dot_general | solution.py:62
  (4 shorter events, 0.1 us)
Async XLA Ops:
  6.5 125.6 %all-gather.2.cloned.1.call-start = ((), (), s32[]{:S(2)}) async-start(), calls=%async_computation.1 | async-start | bytes 1114112 | tf_op jit(solution)/shard_map/all_gather | solution.py:61
  6.5 10.9 %collective-permute-start = (f32[8,11392]{1,0:T(8,128)}, f32[8,11392]{1,0:T(8,128)S(1)}, u32[]{:S(2)}, u32[]{:S(2)}) collective-permute-start(f32[8,11392]{1,0:T(8,128)} %param.5), channel_id=1, source_target_pairs={{0,1},{1,2},{2,3},{3,4},{4,5},{5,6},{6,7},{7,8},{8,9},{9,10},{10,1... | collective-permute-start | bytes 1093640 | tf_op jit(solution)/shard_map/ppermute | solution.py:19
  8.9 9.6 %collective-permute-start.1 = (f32[8,11392]{1,0:T(8,128)}, f32[8,11392]{1,0:T(8,128)S(1)}, u32[]{:S(2)}, u32[]{:S(2)}) collective-permute-start(f32[8,11392]{1,0:T(8,128)} %param.5), channel_id=1, source_target_pairs={{1,0},{2,1},{3,2},{4,3},{5,4},{6,5},{7,6},{8,7},{9,8},{10,9},{11,1... | collective-permute-start | bytes 1093640 | tf_op jit(solution)/shard_map/ppermute | solution.py:21
Sparse Core Ops, SparseCore 0:
  95.8 36.2 all-gather.1
where the time goes:
time: 152 us
  blocking collectives  76.2 us (50%)
  waiting for transfers between devices  23.6 us (16%)
  between operations  16.1 us (11%)
  other arithmetic  15.1 us (10%)
  matrix products  12.7 us (8%)
  local copies, waits for them, and re-layouts  4.28 us (3%)
  starting transfers between devices  3.66 us (2%)
    psum x1, blocking collectives, body(): spread = lax.psum(jnp.sum(centered * centered, axis=0), ('row', 'col'))  63.9 us
    all_gather x1, waiting for transfers between devices, body(): band_cols = lax.all_gather(band_slice, ('row', 'col'), axis=0, tiled=True)  23.6 us
    dot_general x1, matrix products, body(): lax.dot_general(band_cols, columns, (((0,), (0,)), ((), ())), preferred_e...  12.7 us
    reduce_sum x1, other arithmetic, body(): spread = lax.psum(jnp.sum(centered * centered, axis=0), ('row', 'col'))  12.4 us
    all_to_all x1, blocking collectives, body(): lax.all_to_all(scaled, ('row', 'col'), split_axis=1, concat_axis=0, tiled...  12.3 us
  transfers between devices with their start and end apart: 3, of which 1 were waited for; matrix products, arithmetic and copies ran while one was open for 4% of the time, Pallas kernels for 0%

commit v1 on v0

--- a/solution.py
+++ b/solution.py
@@ -1,3 +1,4 @@
+import functools
 import jax
 import jax.numpy as jnp
 from jax import lax
@@ -6,6 +7,14 @@
 B = 4096
 EPSILON = 1e-06
 CLIP_LIMIT = 0.999
+
+
+def series_all_mix(local_values, axis_name, dev_axis):
+    part_now = jax.lax.psum(jax.lax.psum(local_values, axis_name=axis_name), axis_name=dev_axis)
+    return part_now
+
+
+switch_chains = functools.partial(series_all_mix, axis_name="col", dev_axis="row")
 
 
 def with_halo(cells, sides, width):
@@ -54,7 +63,7 @@
     own_kept = kept_frames[lax.axis_index(("row", "col"))]
     keep_mask = (jnp.arange(block_len, dtype=jnp.int32) < own_kept).astype(jnp.float32)[:, None]
     centered = keep_mask * filtered
-    spread = lax.psum(jnp.sum(centered * centered, axis=0), ("row", "col"))
+    spread = switch_chains(jnp.sum(centered * centered, axis=0))
     scaled = (centered * lax.rsqrt(spread + EPSILON)).astype(jnp.bfloat16)
     columns = lax.all_to_all(scaled, ("row", "col"), split_axis=1, concat_axis=0, tiled=True)
     band_slice = lax.dynamic_slice_in_dim(scaled, band_start[0], B, 1)

time: 152 us -> 133 us (0.88)
  blocking collectives: 76.2 us -> 57 us
    psum x1 -> x2, blocking collectives: 63.9 us -> 44.7 us  [the longest x1 38.1 us: series_all_mix(): jax.lax.psum(jax.lax.psum(local_values, axis_name=axis_name), axis_name=d...]
where the time goes in v1:
time: 133 us; the launch traced here: 132 us
  blocking collectives  57 us (43%)
  waiting for transfers between devices  23.6 us (18%)
  between operations  16.1 us (12%)
  other arithmetic  15.1 us (11%)
  matrix products  12.7 us (10%)
  local copies, waits for them, and re-layouts  4.28 us (3%)
  starting transfers between devices  3.66 us (3%)
    psum x1, blocking collectives, series_all_mix(): jax.lax.psum(jax.lax.psum(local_values, axis_name=axis_name), axis_name=d...  38.1 us
    all_gather x1, waiting for transfers between devices, body(): band_cols = lax.all_gather(band_slice, ('row', 'col'), axis=0, tiled=True)  23.6 us
    dot_general x1, matrix products, body(): lax.dot_general(band_cols, columns, (((0,), (0,)), ((), ())), preferred_e...  12.7 us
    reduce_sum x1, other arithmetic, body(): spread = switch_chains(jnp.sum(centered * centered, axis=0))  12.4 us
    all_to_all x1, blocking collectives, body(): lax.all_to_all(scaled, ('row', 'col'), split_axis=1, concat_axis=0, tiled...  12.3 us
    psum x1, blocking collectives, series_all_mix(): jax.lax.psum(local_values, axis_name=axis_name)  6.59 us
  transfers between devices with their start and end apart: 3, of which 1 were waited for; matrix products, arithmetic and copies ran while one was open for 4% of the time, Pallas kernels for 0%

profile of v1, /device:TPU:0, one launch (start us, length us, event | category | flops | bytes accessed | tf_op | source)
XLA Modules:
  0.0 132.4 jit_solution(17430491446508163915)
XLA Ops:
  6.5 0.0 all-gather.2.cloned.1.call-start
  6.5 2.4 %collective-permute-start = (f32[8,11392]{1,0:T(8,128)}, f32[8,11392]{1,0:T(8,128)S(1)}, u32[]{:S(2)}, u32[]{:S(2)}) collective-permute-start(f32[8,11392]{1,0:T(8,128)} %param.5), channel_id=1, source_target_pairs={{0,1},{1,2},{2,3},{3,4},{4,5},{5,6},{6,7},{7,8},{8,9},{9,10},{10,1... | collective-permute-start | bytes 1093640 | tf_op jit(solution)/shard_map/ppermute | solution.py:28
  8.9 1.3 collective-permute-start.1
  10.9 1.3 dynamic_slice.6
  12.1 1.3 %convert_reduce_fusion = (f32[]{:T(128)}, f32[]{:T(128)}) fusion(s32[]{:T(128)} %bitcast.26, f32[17]{0:T(128)} %param.6), kind=kLoop, calls=%fused_computation.42 | loop fusion | flops 117 | bytes 80 | tf_op jit(solution)/shard_map/reduce_sum | solution.py:41
  13.5 0.6 compare_convert_fusion
  16.1 0.7 subtract_select_fusion
  16.7 0.7 fusion.19
  17.4 0.0 collective-permute-done
  17.5 1.0 constant_dynamic-update-slice_fusion
  18.5 0.0 collective-permute-done.1
  18.6 12.4 %multiply_reduce_fusion = (f32[11392]{0:T(1024)S(1)}, f32[8,11392]{1,0:T(8,128)S(1)}) fusion(f32[8,11392]{1,0:T(8,128)S(1)} %collective-permute-done.1, f32[]{:T(128)} %bitcast.18, f32[16,11392]{1,0:T(8,128)S(1)} %constant_dynamic-update-slice_fusion.2, f32[]{:T(128)} %bitcast.17, f32[]{:T(128)} %bitcast.16, f32[]{:T(128)} %bitcast.15, f32[]{:T(128)} %bitcast.14, ...), kind=kLoop, calls=%fused_computation.33 | loop fusion | flops 3269504 | bytes 6607460 | tf_op jit(solution)/shard_map/reduce_sum | solution.py:66
  31.0 6.6 %psum.14 = f32[11392]{0:T(1024)S(1)} all-reduce(f32[11392]{0:T(1024)S(1)} %get-tuple-element.5), channel_id=1, replica_groups=mesh['subj'=2,'row'=8,'col'=2] {'col'}, use_global_device_ids=true, to_apply=%region_3.0 | all-reduce | flops 11392 | bytes 91136 | tf_op jit(solution)/shard_map/psum | solution.py:13
  37.5 38.1 %psum.15 = f32[11392]{0:T(1024)S(1)} all-reduce(f32[11392]{0:T(1024)S(1)} %psum.14), channel_id=1, replica_groups=mesh['subj'=2,'row'=8,'col'=2] {'row'}, use_global_device_ids=true, to_apply=%region_4.0 | all-reduce | flops 11392 | bytes 91136 | tf_op jit(solution)/shard_map/psum | solution.py:13
  75.7 0.7 constant_dynamic-slice_fusion
  76.5 0.0 all-gather.2.cloned.1.call-update
  76.5 0.4 all_to_all.14
  76.9 0.1 copy.6
  77.0 12.3 %all_to_all.19 = bf16[8,16,712]{2,0,1:T(8,128)(2,1)S(1)} all-to-all(bf16[8,16,712]{2,0,1:T(8,128)(2,1)S(1)} %copy.6), channel_id=1, replica_groups=mesh['subj'=2,'row'=8,'col'=2] {'row','col'}, dimensions={1} | all-to-all | bytes 364544 | tf_op jit(solution)/shard_map/all_to_all | solution.py:68
  89.3 23.6 %all-gather.2.cloned.1.call-done = bf16[128,4096]{1,0:T(8,128)(2,1)} async-done(((bf16[8,4096]{1,0:T(8,128)(2,1)}), bf16[128,4096]{1,0:T(8,128)(2,1)}) %all-gather.2.cloned.1.call-update) | async-done | bytes 1048592 | tf_op jit(solution)/shard_map/all_gather | solution.py:70
  112.9 12.7 %multiply_convert_fusion = bf16[4096,712]{0,1:T(8,128)(2,1)} fusion(bf16[128,4096]{1,0:T(8,128)(2,1)} %all-gather.2.cloned.1.call-done, bf16[8,16,712]{2,0,1:T(8,128)(2,1)S(1)} %all_to_all.19), kind=kOutput, calls=%fused_computation | convolution fusion | flops 761167872 | bytes 7063552 | tf_op jit(solution)/shard_map/dot_general | solution.py:71
  (4 shorter events, 0.1 us)
Async XLA Ops:
  6.5 106.4 %all-gather.2.cloned.1.call-start = ((), (), s32[]{:S(2)}) async-start(), calls=%async_computation.1 | async-start | bytes 1114112 | tf_op jit(solution)/shard_map/all_gather | solution.py:70
  6.5 10.9 %collective-permute-start = (f32[8,11392]{1,0:T(8,128)}, f32[8,11392]{1,0:T(8,128)S(1)}, u32[]{:S(2)}, u32[]{:S(2)}) collective-permute-start(f32[8,11392]{1,0:T(8,128)} %param.5), channel_id=1, source_target_pairs={{0,1},{1,2},{2,3},{3,4},{4,5},{5,6},{6,7},{7,8},{8,9},{9,10},{10,1... | collective-permute-start | bytes 1093640 | tf_op jit(solution)/shard_map/ppermute | solution.py:28
  8.9 9.6 %collective-permute-start.1 = (f32[8,11392]{1,0:T(8,128)}, f32[8,11392]{1,0:T(8,128)S(1)}, u32[]{:S(2)}, u32[]{:S(2)}) collective-permute-start(f32[8,11392]{1,0:T(8,128)} %param.5), channel_id=1, source_target_pairs={{1,0},{2,1},{3,2},{4,3},{5,4},{6,5},{7,6},{8,7},{9,8},{10,9},{11,1... | collective-permute-start | bytes 1093640 | tf_op jit(solution)/shard_map/ppermute | solution.py:30
Sparse Core Ops, SparseCore 0:
  76.6 36.2 all-gather.1
